TPU v7x, 768 devices: a whole 4x8x12 slice. The times are simulated.
768 devices in a mesh: ctx: 96 (over z, y), fsdp: 8 (over x, core).
Axes of the slice: x: 4, y: 8, z: 12, core: 2. Of those that a mesh axis runs over, the one named last changes fastest.
Arguments:
- values: bfloat16 [8, 12288, 4096], P('fsdp', 'ctx'), may hold values from -6 to 6
- cotangent: bfloat16 [8, 12288, 4096], P('fsdp', 'ctx'), may hold values from -6 to 6
- seg_ids: int32 [8, 12288], P('fsdp', 'ctx'), may hold values from 0 to 3, never falling along the last dimension, each value on 1 to 6144 neighbouring positions
- filters: bfloat16 [256, 128], P('fsdp'), may hold values from -0.5 to 0.5
- skip_gain: bfloat16 [4096], P('fsdp'), may hold values from -4 to 4
Outputs:
- mixed: bfloat16 [8, 12288, 4096], P('fsdp', 'ctx')
- grad_values: bfloat16 [8, 12288, 4096], P('fsdp', 'ctx')
- grad_filters: float32 [256, 128], P('fsdp')
- grad_skip: float32 [4096], P('fsdp')
Inputs may be any that keep to these rules, and one draw needn't show every extreme that they name: `seg_ids`: along each stream document numbers start at 0 and never fall; each document covers 1 to 6144 positions, and one covers exactly that many.
All inputs are finite; a program needn't handle non-finite values.
Results may differ from a plain program's by a relative error of at most 0.001.
Values may be sent and summed in bfloat16 or wider, within the bound.
A program may use at most 64 MiB of HBM per device.

v0:
```python
import jax
import jax.numpy as jnp
from jax import lax
from jax.sharding import PartitionSpec as P


def shifted(value, axis, by):
    peers = lax.axis_size(axis)
    pairs = [(i, i + by) for i in range(peers) if 0 <= i + by < peers]
    return lax.ppermute(value, axis, pairs)


def toeplitz(pattern, rows, width):
    count = pattern.shape[0]
    tiled = jnp.broadcast_to(pattern[:, None, :], (count, rows, width + 1)).reshape(
        count, rows * (width + 1)
    )
    return tiled[:, : rows * width].reshape(count, rows, width)


def diagonals(matrix, taps):
    count, rows, width = matrix.shape
    flat = jnp.concatenate(
        [matrix.reshape(count, rows * width), jnp.zeros((count, rows), matrix.dtype)], axis=1
    )
    bands = flat.reshape(count, rows, width + 1)[:, :, 1 : taps + 1]
    return jnp.sum(bands, axis=1)[:, ::-1]


def shards(values, cotangent, seg_ids, filters, skip_gain):
    local_vals = values[0]
    local_cot = cotangent[0]
    local_ids = seg_ids[0]
    rows, channels = local_vals.shape
    taps = filters.shape[1]
    filt, skip = (
        lax.all_gather(filters, "fsdp", axis=0, tiled=True),
        lax.all_gather(skip_gain, "fsdp", axis=0, tiled=True),
    )
    groups = filt.shape[0]
    gsize = channels // groups
    width = rows + taps
    tail_vals, tail_ids = shifted((local_vals, local_ids), "ctx", 1)
    vals_ext = jnp.concatenate([tail_vals, local_vals], axis=0)
    ids_prev = jnp.concatenate([tail_ids, local_ids], axis=0)
    same_prev = local_ids[:, None] == ids_prev[None, :]
    mask_half = same_prev.astype(jnp.bfloat16)
    mask_full = same_prev.astype(jnp.float32)
    block = min(64, groups)
    span = block * gsize
    skip_full = skip.astype(jnp.float32)
    row_block = max(min(32, rows), rows // 4)

    def one_block(index, carry):
        mixed_buf, adj_buf, fgrad, sgrad = carry
        first = index * block
        column = first * gsize
        fblk = lax.dynamic_slice_in_dim(filt, first, block, 0)
        lead = jnp.concatenate(
            [
                jnp.zeros((block, 1), jnp.bfloat16),
                fblk[:, ::-1],
                jnp.zeros((block, width - taps), jnp.bfloat16),
            ],
            axis=1,
        )
        forward = toeplitz(lead, rows, width) * mask_half[None]
        vblk = lax.dynamic_slice_in_dim(vals_ext, column, span, 1).reshape(width, block, gsize)
        own_vals = lax.dynamic_slice_in_dim(local_vals, column, span, 1)
        own_cot = lax.dynamic_slice_in_dim(local_cot, column, span, 1)
        cblk = own_cot.reshape(rows, block, gsize)
        skip_blk = lax.dynamic_slice_in_dim(skip_full, column, span, 0)
        conv = jnp.einsum(
            "gts,sgc->tgc", forward, vblk, preferred_element_type=jnp.float32
        ).reshape(rows, span)
        mixed_blk = (conv + skip_blk[None, :] * own_vals.astype(jnp.float32)).astype(jnp.bfloat16)
        skip_term = skip_blk[None, :] * own_cot.astype(jnp.float32)
        adj_blk = jnp.einsum(
            "gts,tgc->sgc", forward, cblk, preferred_element_type=jnp.float32
        ).reshape(width, span)
        adj_blk = adj_blk.at[taps:].add(skip_term)
        fsum = jnp.zeros((block, taps), jnp.float32)
        for offset in range(0, rows, row_block):
            cot_part = cblk[offset : offset + row_block]
            val_part = vblk[offset : offset + row_block + taps]
            mask_part = mask_full[offset : offset + row_block, offset : offset + row_block + taps]
            prod = (
                jnp.einsum("tgc,sgc->gts", cot_part, val_part, preferred_element_type=jnp.float32)
                * mask_part[None]
            )
            fsum = fsum + diagonals(prod, taps)
        mixed_buf = lax.dynamic_update_slice_in_dim(mixed_buf, mixed_blk, column, 1)
        adj_buf = lax.dynamic_update_slice_in_dim(adj_buf, adj_blk, column, 1)
        fgrad = lax.dynamic_update_slice_in_dim(fgrad, fsum, first, 0)
        sgrad = lax.dynamic_update_slice_in_dim(
            sgrad,
            jnp.sum(own_cot.astype(jnp.float32) * own_vals.astype(jnp.float32), axis=0),
            column,
            0,
        )
        return (mixed_buf, adj_buf, fgrad, sgrad)

    init = (
        jnp.zeros((rows, channels), jnp.bfloat16),
        jnp.zeros((width, channels), jnp.float32),
        jnp.zeros((groups, taps), jnp.float32),
        jnp.zeros((channels,), jnp.float32),
    )
    mixed_buf, adj_buf, fgrad, sgrad = lax.fori_loop(0, groups // block, one_block, init)
    spill = shifted(adj_buf[:taps], "ctx", -1)
    adjoint = adj_buf[taps:].at[rows - taps :].add(spill)
    grad_vals = adjoint.astype(jnp.bfloat16)
    shard_f, shard_s = (
        lax.psum_scatter(fgrad, "fsdp", scatter_dimension=0, tiled=True),
        lax.psum_scatter(sgrad, "fsdp", scatter_dimension=0, tiled=True),
    )
    total_f, total_s = lax.psum((shard_f, shard_s), "ctx")
    stream_count = lax.axis_size("fsdp")
    seq_length = rows * lax.axis_size("ctx")
    total_f = total_f / jnp.sqrt(jnp.float32(stream_count * seq_length * gsize))
    total_s = total_s / jnp.sqrt(jnp.float32(stream_count * seq_length))
    return (mixed_buf[None], grad_vals[None], total_f, total_s)


def solution(mesh):
    placed = (
        P("fsdp", "ctx", None),
        P("fsdp", "ctx", None),
        P("fsdp", "ctx"),
        P("fsdp", None),
        P("fsdp"),
    )
    return jax.shard_map(
        shards,
        mesh=mesh,
        in_specs=placed,
        out_specs=(P("fsdp", "ctx", None), P("fsdp", "ctx", None), P("fsdp", None), P("fsdp")),
        check_vma=False,
    )
```

profile of v0, /device:TPU:2, one launch (start us, length us, event | category | flops | bytes accessed | tf_op | source)
XLA Modules:
  0.0 772.3 jit_solution(9427307171723863192)
XLA Ops:
  7.2 2.3 copy.19
  9.6 3.5 collective-permute-start
  13.1 3.4 collective-permute-start.1
  16.6 15.8 %all_gather.6 = bf16[256,128]{1,0:T(8,128)(2,1)} all-gather(bf16[32,128]{1,0:T(8,128)(2,1)S(1)} %copy-done.5), channel_id=1, replica_groups=mesh['ctx'=96,'fsdp'=8] {'fsdp'}, dimensions={0}, use_global_device_ids=true | all-gather | bytes 73728 | tf_op jit(solution)/shard_map/all_gather | solution.py:37
  32.4 12.2 %all-gather = bf16[8,1,512]{2,1,0:T(2,128)(2,1)S(1)} all-gather(bf16[1,1,512]{2,1,0:T(2,128)(2,1)S(1)} %reshape.284), channel_id=1, replica_groups=mesh['ctx'=96,'fsdp'=8] {'fsdp'}, dimensions={0}, use_global_device_ids=true | all-gather | bytes 9216 | tf_op jit(solution)/shard_map/all_gather | solution.py:38
  50.1 2.6 broadcast_in_dim.58.clone
  55.0 241.8 %while.25 = (s32[]{:T(128)}, bf16[128,4096]{1,0:T(8,128)(2,1)}, f32[256,4096]{1,0:T(8,128)}, f32[256,128]{1,0:T(8,128)}, f32[4096]{0:T(1024)}, /*index=5*/bf16[2...) while((s32[]{:T(128)}, bf16[128,4096]{1,0:T(8,128)(2,1)}, ...), condition=%wide.region_6.7_spmd.clone, body=%wide.region_0.6_spmd.clone.sunk | while | flops 182082944 | bytes 126698264 | solution.py:109
  55.0 2.0 fusion.61
  57.0 2.6 fusion.60
  62.8 2.9 reshape.315
  70.0 2.9 reshape.317
  76.7 2.9 reshape.319
  83.4 2.9 reshape.321
  89.4 3.2 broadcast_in_dim.65
  92.6 10.8 %reshape.313 = bf16[64,32896]{1,0:T(8,128)(2,1)} reshape(bf16[64,128,257]{2,1,0:T(8,128)(2,1)} %broadcast_in_dim.65) | data formatting | bytes 8421376 | tf_op jit(solution)/shard_map/while/body/eval_jaxpr/reshape | solution.py:15
  103.4 2.2 slice-done
  115.5 2.0 fusion.61
  117.5 2.7 fusion.60
  123.4 2.9 reshape.315
  130.6 2.9 reshape.317
  137.3 2.9 reshape.319
  143.9 2.9 reshape.321
  150.0 3.2 broadcast_in_dim.65
  153.2 10.8 %reshape.313 = bf16[64,32896]{1,0:T(8,128)(2,1)} reshape(bf16[64,128,257]{2,1,0:T(8,128)(2,1)} %broadcast_in_dim.65) | data formatting | bytes 8421376 | tf_op jit(solution)/shard_map/while/body/eval_jaxpr/reshape | solution.py:15
  164.0 2.2 slice-done
  176.0 2.0 fusion.61
  178.0 2.6 fusion.60
  183.8 2.9 reshape.315
  191.1 2.9 reshape.317
  197.7 2.9 reshape.319
  204.4 2.9 reshape.321
  210.4 3.2 broadcast_in_dim.65
  213.6 10.8 %reshape.313 = bf16[64,32896]{1,0:T(8,128)(2,1)} reshape(bf16[64,128,257]{2,1,0:T(8,128)(2,1)} %broadcast_in_dim.65) | data formatting | bytes 8421376 | tf_op jit(solution)/shard_map/while/body/eval_jaxpr/reshape | solution.py:15
  224.4 2.2 slice-done
  236.4 2.0 fusion.61
  238.5 2.6 fusion.60
  244.2 2.9 reshape.315
  251.5 2.9 reshape.317
  258.1 2.9 reshape.319
  264.8 2.9 reshape.321
  270.8 3.2 broadcast_in_dim.65
  274.0 10.8 %reshape.313 = bf16[64,32896]{1,0:T(8,128)(2,1)} reshape(bf16[64,128,257]{2,1,0:T(8,128)(2,1)} %broadcast_in_dim.65) | data formatting | bytes 8421376 | tf_op jit(solution)/shard_map/while/body/eval_jaxpr/reshape | solution.py:15
  284.8 2.2 slice-done
  296.8 3.2 slice.251
  303.2 22.6 %all-reduce.4 = f32[4096]{0:T(1024)S(1)} all-reduce(f32[4096]{0:T(1024)S(1)} %copy-done.4), channel_id=3, replica_groups=mesh['ctx'=96,'fsdp'=8] {'fsdp'}, use_global_device_ids=true, to_apply=%region_9.0.clone | all-reduce | flops 4096 | bytes 32768
  325.9 16.4 %reduce-scatter.2.cloned.1.call-done = f32[32,128]{1,0:T(8,128)} async-done(((f32[256,128]{1,0:T(8,128)}), f32[32,128]{1,0:T(8,128)}) %reduce-scatter.2.cloned.1.call-update) | async-done | bytes 16400 | tf_op jit(solution)/shard_map/reduce_scatter | solution.py:114
  342.3 419.2 %all-reduce.5 = (f32[32,128]{1,0:T(8,128)S(1)}, f32[512]{0:T(512)S(1)}) all-reduce(f32[32,128]{1,0:T(8,128)} %reduce-scatter.2.cloned.1.call-done, f32[512]{0:T(512)S(1)} %dynamic-slice.23), channel_id=1, replica_groups=mesh['ctx'=96,'fsdp'=8] {'ctx'}, use_global_device_ids=true, to_apply=%region_8.0 | all-reduce | flops 4608 | bytes 36864 | tf_op jit(solution)/shard_map/psum | solution.py:117
  762.7 2.8 fusion.7
  (227 shorter events, 123.3 us)
Async XLA Ops:
  7.2 9.4 %copy-start.6 = (bf16[512]{0:T(512)(128)(2,1)S(1)}, bf16[512]{0:T(512)(128)(2,1)}, u32[]{:S(2)}) copy-start(bf16[512]{0:T(512)(128)(2,1)} %param.17) | copy-start | bytes 3076
  7.2 9.4 %copy-start.5 = (bf16[32,128]{1,0:T(8,128)(2,1)S(1)}, bf16[32,128]{1,0:T(8,128)(2,1)}, u32[]{:S(2)}) copy-start(bf16[32,128]{1,0:T(8,128)(2,1)} %param.16) | copy-start | bytes 24580
  7.2 37.4 %copy-start.3 = (bf16[1,128,4096]{2,1,0:T(8,128)(2,1)S(1)}, bf16[1,128,4096]{2,1,0:T(8,128)(2,1)}, u32[]{:S(2)}) copy-start(bf16[1,128,4096]{2,1,0:T(8,128)(2,1)} %param.14) | copy-start | bytes 3145732
  7.2 335.1 %reduce-scatter.2.cloned.1.call-start = ((), (), s32[]{:S(2)}) async-start(), calls=%async_computation.1 | async-start | bytes 147456 | tf_op jit(solution)/shard_map/reduce_scatter | solution.py:114
  9.6 39.0 %collective-permute-start = (bf16[128,4096]{0,1:T(8,128)(2,1)}, bf16[128,4096]{0,1:T(8,128)(2,1)S(1)}, u32[]{:S(2)}, u32[]{:S(2)}) collective-permute-start(bf16[128,4096]{0,1:T(8,128)(2,1)} %bitcast), channel_id=1, source_target_pairs={{0,8},{8,16},{16,24},{24,32},{32,40},{40,48},{48,56},{56,64},{64,7... | collective-permute-start | bytes 3145736 | tf_op jit(solution)/shard_map/ppermute | solution.py:10
  13.1 32.8 %collective-permute-start.1 = (s32[128]{0:T(128)}, s32[128]{0:T(128)S(1)}, u32[]{:S(2)}, u32[]{:S(2)}) collective-permute-start(s32[128]{0:T(128)} %bitcast.3), channel_id=1, source_target_pairs={{0,8},{8,16},{16,24},{24,32},{32,40},{40,48},{48,56},{56,64},{64,7... | collective-permute-start | bytes 1544 | tf_op jit(solution)/shard_map/ppermute | solution.py:10
  55.0 2.0 copy-start
  83.4 3.3 copy-start.2
  103.4 2.2 slice-start
  112.0 3.5 copy-start.1
  115.5 2.0 copy-start
  143.9 3.3 copy-start.2
  164.0 2.2 slice-start
  172.6 3.4 copy-start.1
  176.0 2.0 copy-start
  204.4 3.3 copy-start.2
  224.4 2.2 slice-start
  233.0 3.4 copy-start.1
  236.4 2.0 copy-start
  264.8 3.3 copy-start.2
  284.8 2.2 slice-start
  293.4 3.4 copy-start.1
  296.8 6.4 copy-start.4
  300.0 462.7 %collective-permute-start.2 = (f32[128,4096]{1,0:T(8,128)}, f32[128,4096]{1,0:T(8,128)S(1)}, u32[]{:S(2)}, u32[]{:S(2)}) collective-permute-start(f32[128,4096]{1,0:T(8,128)} %slice.251), channel_id=1, source_target_pairs={{8,0},{16,8},{24,16},{32,24},{40,32},{48,40},{56,48},{64,56},{72,6... | collective-permute-start | bytes 6291464 | tf_op jit(solution)/shard_map/ppermute | solution.py:10
Sparse Core Ops, SparseCore 0:
  301.4 40.8 reduce-scatter.1
where the time goes:
time: 775 us; the launch traced here: 772 us
  blocking collectives  470 us (61%)
  local copies, waits for them, and re-layouts  205 us (26%)
  matrix products  28.9 us (4%)
  other arithmetic  28.6 us (4%)
  waiting for transfers between devices  16.4 us (2%)
  between operations  14.8 us (2%)
  starting transfers between devices  8.27 us (1%)
    psum x1, blocking collectives, shards(): total_f, total_s = lax.psum((shard_f, shard_s), 'ctx')  419 us
    reshape x16, local copies, waits for them, and re-layouts, diagonals(): bands = flat.reshape(count, rows, width + 1)[:, :, 1:taps + 1]  45.7 us
    reshape x4, local copies, waits for them, and re-layouts, toeplitz(): jnp.broadcast_to(pattern[:, None, :], (count, rows, width + 1))  43.3 us
    reshape x16, local copies, waits for them, and re-layouts, diagonals(): matrix.reshape(count, rows * width)  26.1 us
    unnamed x1, blocking collectives  22.6 us
    dot_general x16, matrix products, one_block(): jnp.einsum('tgc,sgc->gts', cot_part, val_part, preferred_element_type=jnp...  21.4 us
    reduce_scatter x1, waiting for transfers between devices, shards(): lax.psum_scatter(fgrad, 'fsdp', scatter_dimension=0, tiled=True)  16.4 us
    all_gather x1, blocking collectives, shards(): lax.all_gather(filters, 'fsdp', axis=0, tiled=True)  15.8 us
  transfers between devices with their start and end apart: 4, of which 1 were waited for; matrix products, arithmetic and copies ran while one was open for 1% of the time, Pallas kernels for 0%

commit v1 on v0

v1 whole, which is shorter than its diff:
```python
import functools

import jax
import jax.numpy as jnp
from jax import lax
from jax.experimental import pallas as pl
from jax.experimental.pallas import tpu as pltpu
from jax.sharding import PartitionSpec as P

MESH = pl.DeviceIdType.MESH
LANES = 128
BLOCK = 256
F32 = jnp.float32
BF16 = jnp.bfloat16


def divide(extent, unit):
    return (extent + unit - 1) // unit


def kernel(
    sizes,
    values, cotangent, ids, filt, skip,
    mixed, gvals, fgrad, sgrad,
    v1, c1, v0, c2, mix_buf, adj_buf, ids_prev, ids_next, filt_all, skip_all,
    taps_buf, base_f, base_a, mask_f, mask_a, mask_g, lhs_f, lhs_a, lhs_g, row_acc,
    part, part_in, y_in, z_in, z_own, y_own, final,
    load_sem, store_sem, halo_send, halo_recv, ids_send, ids_recv, filt_send, filt_recv,
    skip_send, skip_recv, part_send, part_recv, y_send, y_recv, z_send, z_recv, g_send, g_recv,
):
    ring, fs, ny, f_scale, s_scale = sizes
    nz = ring // ny
    rows = v1.shape[0]
    width = v1.shape[1] // fs
    groups = filt.shape[0]
    gsize = width // groups
    per_block = BLOCK // gsize
    blocks = width // BLOCK
    piece = part.shape[1] // ny
    grows = groups // ny
    srow_all = width // LANES
    ctx = lax.axis_index("ctx")
    me = lax.axis_index("fsdp")
    zz, yy = ctx // ny, lax.rem(ctx, ny)
    ahead, behind = lax.rem(ctx + 1, ring), lax.rem(ctx + ring - 1, ring)

    def chunk_of(k):
        return lax.rem(me + 1 + k, fs)

    def columns(k):
        return pl.ds(pl.multiple_of(chunk_of(k) * width, width), width)

    loads = [
        pltpu.make_async_copy(values.at[0], v1, load_sem.at[0]),
        pltpu.make_async_copy(cotangent.at[0], c1, load_sem.at[1]),
    ]
    for load in loads:
        load.start()

    barrier = pltpu.get_barrier_semaphore()
    peers = [(ahead, me), (behind, me)]
    peers += [(ctx, lax.rem(me + d, fs)) for d in range(1, fs)]
    peers += [(zz * ny + lax.rem(yy + d, ny), me) for d in range(1, ny)]
    peers += [(lax.rem(zz + d, nz) * ny + yy, me) for d in range(1, nz)]
    for peer in peers:
        pl.semaphore_signal(barrier, inc=1, device_id=peer, device_id_type=MESH)
    pl.semaphore_wait(barrier, len(peers))

    def remote(src, dst, send, recv, peer):
        return pltpu.make_async_remote_copy(
            src_ref=src, dst_ref=dst, send_sem=send, recv_sem=recv,
            device_id=peer, device_id_type=MESH,
        )

    def filt_copy(d):
        return remote(filt, filt_all.at[me], filt_send.at[d - 1], filt_recv.at[d - 1],
                      (ctx, lax.rem(me + d, fs)))

    def skip_copy(d):
        return remote(skip, skip_all.at[me], skip_send.at[d - 1], skip_recv.at[d - 1],
                      (ctx, lax.rem(me + d, fs)))

    def vals_copy(k):
        return remote(values.at[0, :, columns(k)], v0.at[:, columns(k)],
                      halo_send.at[0, k], halo_recv.at[0, k], (ahead, me))

    def cots_copy(k):
        return remote(cotangent.at[0, :, columns(k)], c2.at[:, columns(k)],
                      halo_send.at[1, k], halo_recv.at[1, k], (behind, me))

    def part_copy(k):
        return remote(part.at[k], part_in.at[k], part_send.at[k], part_recv.at[k],
                      (ctx, chunk_of(k)))

    ids_copies = [
        remote(ids, ids_prev, ids_send.at[0], ids_recv.at[0], (ahead, me)),
        remote(ids, ids_next, ids_send.at[1], ids_recv.at[1], (behind, me)),
    ]
    for copy in ids_copies:
        copy.start()
    for d in range(fs - 1, 0, -1):
        filt_copy(d).start()
        skip_copy(d).start()

    def send_halo(k, carry):
        vals_copy(k).start()
        cots_copy(k).start()
        return carry

    lax.fori_loop(0, fs, send_halo, 0)

    filt_all[me] = filt[...]
    skip_all[me] = skip[...]
    row = lax.broadcasted_iota(jnp.int32, (rows, rows), 0)
    lane = lax.broadcasted_iota(jnp.int32, (rows, rows), 1)
    perm = jnp.where(lax.rem(row + lane, rows) == 0, 1.0, 0.0).astype(BF16)
    for copy in ids_copies:
        copy.wait()
    own = jnp.broadcast_to(ids[...].astype(F32), (rows, rows))
    own_col = own.T
    edge_prev = jnp.where(ctx == 0, -1.0, 0.0)
    edge_next = jnp.where(ctx == ring - 1, -1.0, 0.0)
    prev = jnp.broadcast_to(ids_prev[...].astype(F32), (rows, rows))
    prev = jnp.where(edge_prev < 0, -1.0, prev)
    after = jnp.broadcast_to(ids_next[...].astype(F32), (rows, rows))
    after = jnp.where(edge_next < 0, -1.0, after)
    same = own_col == own
    mask_f[:, :rows] = jnp.where(same & (lane <= row), 1.0, 0.0).astype(BF16)
    mask_f[:, rows:] = jnp.where((own_col == prev) & (lane > row), 1.0, 0.0).astype(BF16)
    m1 = jnp.where(same & (lane >= row), 1.0, 0.0)
    m2 = jnp.where((own_col == after) & (lane < row), 1.0, 0.0)
    mask_a[:, :rows] = m1.astype(BF16)
    mask_a[:, rows:] = m2.astype(BF16)
    mask_g[...] = m1 + m2
    upper = lane >= row
    group_lane = lax.broadcasted_iota(jnp.int32, (rows, BLOCK), 1) // gsize
    sub = 16
    steps = rows // sub
    for load in loads:
        load.wait()

    def store_copies(k):
        return (
            pltpu.make_async_copy(
                mix_buf.at[:, columns(k)], mixed.at[0, :, columns(k)], store_sem.at[0, k]),
            pltpu.make_async_copy(
                adj_buf.at[:, columns(k)], gvals.at[0, :, columns(k)], store_sem.at[1, k]),
        )

    def one_chunk(k, carry):
        chunk = chunk_of(k)

        @pl.when(k < fs - 1)
        def _():
            filt_copy(fs - 1 - k).wait_recv()
            skip_copy(fs - 1 - k).wait_recv()

        taps = filt_all[chunk]
        taps_buf[:groups] = jnp.dot(taps, perm, preferred_element_type=F32)
        taps_buf[groups:] = taps.astype(F32)

        def spread(g, inner):
            at = pl.ds(pl.multiple_of(g * sub, sub), sub)
            wide = jnp.broadcast_to(taps_buf[pl.ds(g, 1), :], (sub, rows))
            base_f[at, :] = pltpu.roll(wide, 0, 1, stride=1, stride_axis=0).astype(BF16)
            wide = jnp.broadcast_to(taps_buf[pl.ds(groups + g, 1), :], (sub, rows))
            base_a[at, :] = pltpu.roll(wide, 0, 1, stride=1, stride_axis=0).astype(BF16)
            return inner

        lax.fori_loop(0, groups, spread, 0, unroll=8)
        vals_copy(k).wait_recv()
        cots_copy(k).wait_recv()
        gains = skip_all[chunk].astype(F32)
        for b in range(blocks):
            cs = pl.ds(pl.multiple_of(chunk * width + b * BLOCK, BLOCK), BLOCK)
            vb, cb = v1[:, cs], c1[:, cs]
            wf = jnp.concatenate([vb, v0[:, cs]], axis=0)
            wa = jnp.concatenate([cb, c2[:, cs]], axis=0)
            at = slice(b * per_block * sub, (b + 1) * per_block * sub)
            bf, ba = base_f[at, :], base_a[at, :]
            for s in range(steps):
                here = slice(s * sub, (s + 1) * sub)
                x = (bf if s == 0 else pltpu.roll(bf, s * sub, 1)).reshape(per_block, sub, rows)
                lhs_f[:, here, :rows] = x * mask_f[here, :rows][None]
                lhs_f[:, here, rows:] = x * mask_f[here, rows:][None]
                x = (ba if s == 0 else pltpu.roll(ba, s * sub, 1)).reshape(per_block, sub, rows)
                lhs_a[:, here, :rows] = x * mask_a[here, :rows][None]
                lhs_a[:, here, rows:] = x * mask_a[here, rows:][None]
            for i in range(per_block):
                lhs_g[i] = jnp.where(group_lane == i, vb, jnp.zeros_like(vb))
            flat = (per_block * rows, BLOCK)
            cube = (per_block, rows, BLOCK)
            rf = jnp.dot(lhs_f[...].reshape(flat), wf, preferred_element_type=F32).reshape(cube)
            ra = jnp.dot(lhs_a[...].reshape(flat), wa, preferred_element_type=F32).reshape(cube)
            rg = lax.dot_general(
                lhs_g[...].reshape(flat), wa, (((1,), (1,)), ((), ())), preferred_element_type=F32
            ).reshape(cube)
            vf, cf = vb.astype(F32), cb.astype(F32)
            sums = jnp.sum(vf * cf, axis=0, keepdims=True)
            half = LANES // gsize
            for h in range(BLOCK // LANES):
                ls = slice(h * LANES, (h + 1) * LANES)
                q = b * (BLOCK // LANES) + h
                to = pl.ds(pl.multiple_of(chunk * width + q * LANES, LANES), LANES)
                for result, out, x in ((rf, mix_buf, vf), (ra, adj_buf, cf)):
                    acc = result[h * half, :, ls]
                    for i in range(1, half):
                        acc = jnp.where(group_lane[:, ls] == h * half + i,
                                        result[h * half + i, :, ls], acc)
                    acc = acc + gains[q:q + 1, :] * x[:, ls]
                    out[:, to] = acc.astype(BF16)
                part[k, pl.ds((q % ny) * piece + grows + q // ny, 1), :] = sums[:, ls]
            prod = jnp.where(upper[None], rg[:, :, :rows], rg[:, :, rows:]) * mask_g[...][None]
            acc = prod[:, :8, :].reshape(per_block * 8, rows)
            for s in range(1, rows // 8):
                acc = acc + pltpu.roll(
                    prod[:, 8 * s:8 * s + 8, :].reshape(per_block * 8, rows), rows - 8 * s, 1)
            row_acc[b * per_block * 8:(b + 1) * per_block * 8, :] = acc
        for store in store_copies(k):
            store.start()
        total = row_acc[pl.ds(0, groups, stride=8), :]
        for r in range(1, 8):
            total = total + pltpu.roll(row_acc[pl.ds(r, groups, stride=8), :], rows - r, 1)
        for r in range(grows):
            part[k, pl.ds(r, ny, stride=piece), :] = total[r * ny:(r + 1) * ny]

        @pl.when(k < fs - 1)
        def _():
            part_copy(k).start()

        return carry

    part[...] = jnp.zeros_like(part)
    lax.fori_loop(0, fs, one_chunk, 0)

    total = part[fs - 1]
    for k in range(fs - 1):
        part_copy(k).wait_recv()
        total = total + part_in[k]
    y_own[...] = total

    def y_piece(at):
        return pl.ds(pl.multiple_of(at * piece, piece), piece)

    def y_copy(d):
        to = lax.rem(yy + d, ny)
        return remote(y_own.at[y_piece(to), :], y_in.at[d - 1], y_send.at[d - 1], y_recv.at[d - 1],
                      (zz * ny + to, me))

    def z_copy(d):
        return remote(z_own, z_in.at[zz], z_send.at[d - 1], z_recv.at[d - 1],
                      (lax.rem(zz + d, nz) * ny + yy, me))

    def g_copy(d):
        return remote(final.at[yy], final.at[yy], g_send.at[d - 1], g_recv.at[d - 1],
                      (zz * ny + lax.rem(yy + d, ny), me))

    for d in range(1, ny):
        y_copy(d).start()
    mine = y_own[y_piece(yy), :]
    for d in range(1, ny):
        y_copy(d).wait_recv()
        mine = mine + y_in[d - 1]
    z_own[...] = mine
    for d in range(1, nz):
        z_copy(d).start()
    z_in[zz] = mine
    for d in range(1, nz):
        z_copy(d).wait_recv()
    mine = z_in[0]
    for i in range(1, nz):
        mine = mine + z_in[i]
    piece_row = lax.broadcasted_iota(jnp.int32, mine.shape, 0)
    final[yy] = mine * jnp.where(piece_row < grows, f_scale, s_scale)
    for d in range(1, ny):
        g_copy(d).start()
    for d in range(1, ny):
        g_copy(d).wait_recv()
    for p in range(ny):
        block = final[p]
        fgrad[pl.ds(p, grows, stride=ny), :] = block[:grows]
        for q in range(p, srow_all, ny):
            sgrad[q:q + 1, :] = block[grows + q // ny:grows + q // ny + 1]

    for d in range(1, fs):
        filt_copy(d).wait_send()
        skip_copy(d).wait_send()

    def finish(k, carry):
        vals_copy(k).wait_send()
        cots_copy(k).wait_send()
        for store in store_copies(k):
            store.wait()
        return carry

    lax.fori_loop(0, fs, finish, 0)
    for k in range(fs - 1):
        part_copy(k).wait_send()
    for d in range(1, ny):
        y_copy(d).wait_send()
        g_copy(d).wait_send()
    for d in range(1, nz):
        z_copy(d).wait_send()


def shards(ny, values, cotangent, seg_ids, filters, skip_gain):
    ring, fs = lax.axis_size("ctx"), lax.axis_size("fsdp")
    _, rows, channels = values.shape
    groups = filters.shape[0]
    width = channels // fs
    gsize = width // groups
    lines = width // LANES
    nz = ring // ny
    piece = divide(groups // ny + divide(lines, ny), 8) * 8
    per_block = BLOCK // gsize
    f_scale = 1.0 / float(fs * rows * ring * gsize) ** 0.5
    s_scale = 1.0 / float(fs * rows * ring) ** 0.5
    sizes = (ring, fs, ny, f_scale, s_scale)
    vmem = pltpu.VMEM
    dma = pltpu.SemaphoreType.DMA
    block = vmem((rows, channels), BF16)
    lhs = vmem((per_block, rows, BLOCK), BF16)
    outs = pl.pallas_call(
        functools.partial(kernel, sizes),
        out_shape=(
            jax.ShapeDtypeStruct(values.shape, BF16),
            jax.ShapeDtypeStruct(values.shape, BF16),
            jax.ShapeDtypeStruct((groups, rows), F32),
            jax.ShapeDtypeStruct((lines, LANES), F32),
        ),
        in_specs=[pl.BlockSpec(memory_space=pl.ANY)] * 2
        + [pl.BlockSpec(memory_space=pltpu.VMEM)] * 3,
        out_specs=[pl.BlockSpec(memory_space=pl.ANY)] * 2
        + [pl.BlockSpec(memory_space=pltpu.VMEM)] * 2,
        scratch_shapes=[
            block, block, block, block, block, block,
            vmem((1, rows), jnp.int32), vmem((1, rows), jnp.int32),
            vmem((fs, groups, rows), BF16), vmem((fs, lines, LANES), BF16),
            vmem((2 * groups, rows), F32),
            vmem((groups * 16, rows), BF16), vmem((groups * 16, rows), BF16),
            vmem((rows, BLOCK), BF16), vmem((rows, BLOCK), BF16), vmem((rows, rows), F32),
            lhs, lhs, lhs,
            vmem((groups * 8, rows), F32),
            vmem((fs, ny * piece, LANES), F32), vmem((fs, ny * piece, LANES), F32),
            vmem((ny, piece, LANES), F32), vmem((nz, piece, LANES), F32),
            vmem((piece, LANES), F32), vmem((ny * piece, LANES), F32),
            vmem((ny, piece, LANES), F32),
            dma((2,)), dma((2, fs)), dma((2, fs)), dma((2, fs)), dma((2,)), dma((2,)),
            dma((fs,)), dma((fs,)), dma((fs,)), dma((fs,)), dma((fs,)), dma((fs,)),
            dma((ny,)), dma((ny,)), dma((nz,)), dma((nz,)), dma((ny,)), dma((ny,)),
        ],
        compiler_params=pltpu.CompilerParams(
            collective_id=0, has_side_effects=True, vmem_limit_bytes=56 << 20
        ),
    )(values, cotangent, seg_ids, filters, skip_gain.reshape(lines, LANES))
    mixed, gvals, fgrad, sgrad = outs
    return mixed, gvals, fgrad, sgrad.reshape(width)


def solution(mesh, ny=8):
    placed = (
        P("fsdp", "ctx", None),
        P("fsdp", "ctx", None),
        P("fsdp", "ctx"),
        P("fsdp", None),
        P("fsdp"),
    )
    return jax.shard_map(
        functools.partial(shards, ny),
        mesh=mesh,
        in_specs=placed,
        out_specs=(P("fsdp", "ctx", None), P("fsdp", "ctx", None), P("fsdp", None), P("fsdp")),
        check_vma=False,
    )
```

time: 775 us -> 70.6 us (0.09)
  blocking collectives: 470 us -> 0 us
  local copies, waits for them, and re-layouts: 205 us -> 4.59 us
  Pallas kernels: 0 us -> 65.1 us
  matrix products: 28.9 us -> 0 us
  other arithmetic: 28.6 us -> 0 us
  waiting for transfers between devices: 16.4 us -> 0 us
  between operations: 14.8 us -> 0.65 us
  starting transfers between devices: 8.27 us -> 0 us
    psum x1 -> x0, blocking collectives: 419 us -> none  [shards(): total_f, total_s = lax.psum((shard_f, shard_s), 'ctx')]
    reshape x36 -> x0, local copies, waits for them, and re-layouts: 115 us -> none  [the longest x16 45.7 us: diagonals(): bands = flat.reshape(count, rows, width + 1)[:, :, 1:taps + 1]]
    pallas_call x0 -> x1, Pallas kernels: none -> 65.1 us  [shards(): pl.pallas_call(functools.partial(kernel, sizes), out_shape=(jax.ShapeDtyp...]
    slice x21 -> x0, local copies, waits for them, and re-layouts: 34.1 us -> none  [the longest x4 10.6 us: one_block(): cot_part = cblk[offset:offset + row_block]]
    dot_general x24 -> x0, matrix products: 28.9 us -> none  [the longest x16 21.4 us: one_block(): jnp.einsum('tgc,sgc->gts', cot_part, val_part, preferred_element_type=jnp...]
    all_gather x2 -> x0, blocking collectives: 28 us -> none  [the longest x1 15.8 us: shards(): lax.all_gather(filters, 'fsdp', axis=0, tiled=True)]
    unnamed x1 -> x0, blocking collectives: 22.6 us -> none
    broadcast_in_dim x8 -> x0, local copies, waits for them, and re-layouts: 17.7 us -> none  [the longest x4 12.8 us: toeplitz(): jnp.broadcast_to(pattern[:, None, :], (count, rows, width + 1))]
  transfers between devices with their start and end apart: 4 -> 0, of which waited for: 1 -> 0; matrix products, arithmetic and copies ran while one was open for 1% -> 0% of each run, Pallas kernels for 0% -> 0%
where the time goes in v1:
time: 70.6 us; the launch traced here: 70.3 us
  Pallas kernels  65.1 us (92%)
  local copies, waits for them, and re-layouts  4.59 us (7%)
    pallas_call x1, Pallas kernels, shards(): pl.pallas_call(functools.partial(kernel, sizes), out_shape=(jax.ShapeDtyp...  65.1 us
    unnamed x10, local copies, waits for them, and re-layouts  4.59 us

profile of v1, /device:TPU:2, one launch (start us, length us, event | category | flops | bytes accessed | tf_op | source)
XLA Modules:
  0.0 70.3 jit_solution(4354180089598790445)
XLA Ops:
  0.6 65.1 %shard_map.84 = (bf16[1,128,4096]{2,1,0:T(8,128)(2,1)}, bf16[1,128,4096]{2,1,0:T(8,128)(2,1)}, f32[32,128]{1,0:T(8,128)}, f32[4,128]{1,0:T(4,128)}) custom-call(bf16[1,128,4096]{2,1,0:T(8,128)(2,1)} %values.1, bf16[1,128,4096]{2,1,0:T(8,128)(2,1)} %cotangent.1, s32[1,128]{1,0:T(1,128)} %ids.1, bf16[32,128]{1,0:T(8,128)(2,1)} %filt.1, bf16[4,128]{1,0:T(4,128)(2,1)} %bitcast.3), custom_call_target="tpu_custom_call" | custom-call | tf_op jit(solution)/shard_map/pallas_call | solution.py:323
  65.7 0.0 copy-start
  65.7 2.4 %copy.13 = bf16[1,128,4096]{2,1,0:T(8,128)(2,1)} copy(bf16[1,128,4096]{2,1,0:T(8,128)(2,1)} %get-tuple-element.16) | data formatting | bytes 2097152
  68.1 0.0 copy-done
  68.1 0.0 copy-start.1
  68.1 1.0 %copy.14 = bf16[1,128,4096]{2,1,0:T(8,128)(2,1)} copy(bf16[1,128,4096]{2,1,0:T(8,128)(2,1)S(1)} %copy-done) | data formatting | bytes 2097152
  69.1 0.0 copy-done.1
  69.1 0.0 copy-start.2
  69.1 0.6 copy.15
  69.7 0.1 copy-done.2
  69.8 0.6 copy.16
Async XLA Ops:
  65.7 2.4 %copy-start = (bf16[1,128,4096]{2,1,0:T(8,128)(2,1)S(1)}, bf16[1,128,4096]{2,1,0:T(8,128)(2,1)}, u32[]{:S(2)}) copy-start(bf16[1,128,4096]{2,1,0:T(8,128)(2,1)} %get-tuple-element.17) | copy-start | bytes 3145732
  68.1 1.0 %copy-start.1 = (f32[32,128]{1,0:T(8,128)S(1)}, f32[32,128]{1,0:T(8,128)}, u32[]{:S(2)}) copy-start(f32[32,128]{1,0:T(8,128)} %get-tuple-element.18) | copy-start | bytes 49156
  69.1 0.7 copy-start.2
